TPU v7x, 32 devices: a whole 2x2x4 slice. The times are simulated.
32 devices in a mesh: grp: 2 (over y), col: 4 (over z), seq: 4 (over x, core).
Axes of the slice: x: 2, y: 2, z: 4, core: 2. Of those that a mesh axis runs over, the one named last changes fastest.
Arguments:
- row_query: bfloat16 [256, 16, 768], P(('grp', 'seq'), 'col'), parts along dimension 0, may hold values from -6 to 6
- row_key: bfloat16 [256, 16, 768], P(('grp', 'seq'), 'col'), parts along dimension 0, may hold values from -6 to 6
- row_value: bfloat16 [256, 16, 768], P(('grp', 'seq'), 'col'), parts along dimension 0, may hold values from -6 to 6
- row_grad: bfloat16 [256, 16, 768], P(('grp', 'seq'), 'col'), parts along dimension 0, may hold values from -48 to 48
- col_query: bfloat16 [256, 16, 768], P(('grp', 'seq'), 'col'), parts along dimension 0, may hold values from -11 to 11
- col_key: bfloat16 [256, 16, 768], P(('grp', 'seq'), 'col'), parts along dimension 0, may hold values from -11 to 11
- col_value: bfloat16 [256, 16, 768], P(('grp', 'seq'), 'col'), parts along dimension 0, may hold values from -6 to 6
- col_grad: bfloat16 [256, 16, 768], P(('grp', 'seq'), 'col'), parts along dimension 0, may hold values from -48 to 48
Outputs:
- row_dquery: bfloat16 [256, 16, 768], P(('grp', 'seq'), 'col'), parts along dimension 0
- row_dkey: bfloat16 [256, 16, 768], P(('grp', 'seq'), 'col'), parts along dimension 0
- row_dvalue: bfloat16 [256, 16, 768], P(('grp', 'seq'), 'col'), parts along dimension 0
- col_dquery: bfloat16 [256, 16, 768], P(('grp', 'seq'), 'col'), parts along dimension 0
- col_dkey: bfloat16 [256, 16, 768], P(('grp', 'seq'), 'col'), parts along dimension 0
- col_dvalue: bfloat16 [256, 16, 768], P(('grp', 'seq'), 'col'), parts along dimension 0
There are 2 independent parts, one for each index of `grp`. A program takes and returns all parts, laid end to end along the dimension named above; each array names one. Nothing has to cross between parts.
All inputs are finite; a program needn't handle non-finite values.
Results may differ from a plain program's by a relative error of at most 0.009.
Values may be sent and summed in bfloat16 or wider, within the bound.
No kernel may reach another device: no remote copies, remote signals or barrier semaphores. Data moves between devices by JAX's collectives and lax.ppermute only.
A program may use at most 64 MiB of HBM per device.

v0:
```python
import jax
import jax.numpy as jnp
from jax import lax
from jax.sharding import PartitionSpec as P

HEADS = 12
HEAD = 64


def tied_terms(scores, prob_grad, row_scale):
    row_probs = jax.nn.softmax(scores, axis=-1)
    row_delta = jnp.sum(row_probs * prob_grad, axis=-1, keepdims=True)
    score_gradient_part = row_probs * (prob_grad - row_delta) * row_scale
    return (row_probs.astype(jnp.bfloat16), score_gradient_part.astype(jnp.bfloat16))


def split_heads(block):
    return block.reshape(block.shape[0], block.shape[1] // HEAD, HEAD)


def column_core(query_row_block, key_row_block, value_row_block, gradient_row_block, col_scale):
    scores = (
        jnp.einsum(
            "qzd,izd->zqi", query_row_block, key_row_block, preferred_element_type=jnp.float32
        )
        * col_scale
    )
    prob_grad = jnp.einsum(
        "qzd,izd->zqi", gradient_row_block, value_row_block, preferred_element_type=jnp.float32
    )
    col_probs = jax.nn.softmax(scores, axis=-1)
    col_delta = jnp.sum(col_probs * prob_grad, axis=-1, keepdims=True)
    score_gradient_part = (col_probs * (prob_grad - col_delta) * col_scale).astype(jnp.bfloat16)
    attention_weight_rows = col_probs.astype(jnp.bfloat16)
    query_grad = jnp.einsum(
        "qvc,cqb->vqb", score_gradient_part, key_row_block, preferred_element_type=jnp.float32
    )
    key_gradient_part = jnp.einsum(
        "wzc,zwi->cwi", score_gradient_part, query_row_block, preferred_element_type=jnp.float32
    )
    value_gradient_part = jnp.einsum(
        "wzc,zwi->cwi",
        attention_weight_rows,
        gradient_row_block,
        preferred_element_type=jnp.float32,
    )
    return (
        query_grad.astype(jnp.bfloat16),
        key_gradient_part.astype(jnp.bfloat16),
        value_gradient_part.astype(jnp.bfloat16),
    )


def local(row_query, row_key, row_value, row_grad, col_query, col_key, col_value, col_grad):
    seq_dev, col_dev, width = row_query.shape
    seqs = seq_dev * lax.axis_size("seq")
    cols = col_dev * lax.axis_size("col")
    row_scale = HEAD ** (-0.5) * seqs ** (-0.5)
    col_scale = HEAD ** (-0.5)
    moved = (
        lax.all_to_all(row_query, "col", split_axis=0, concat_axis=1, tiled=True),
        lax.all_to_all(row_key, "col", split_axis=0, concat_axis=1, tiled=True),
        lax.all_to_all(row_value, "col", split_axis=0, concat_axis=1, tiled=True),
        lax.all_to_all(row_grad, "col", split_axis=0, concat_axis=1, tiled=True),
    )
    own_rows = moved[0].shape[0]
    shape_four = (own_rows, cols, HEADS, HEAD)
    query_row_block = moved[0].reshape(shape_four)
    key_row_block = moved[1].reshape(shape_four)
    value_row_block = moved[2].reshape(shape_four)
    gradient_row_block = moved[3].reshape(shape_four)
    score_part = (
        jnp.einsum(
            "sihe,sjhe->hij", query_row_block, key_row_block, preferred_element_type=jnp.float32
        )
        * row_scale
    )
    prob_part = jnp.einsum(
        "sihe,sjhe->hij", gradient_row_block, value_row_block, preferred_element_type=jnp.float32
    )
    scores, prob_grad = lax.psum((score_part, prob_part), ("col", "seq"))
    attention_weight_rows, score_gradient_part = tied_terms(scores, prob_grad, row_scale)
    query_grad = jnp.einsum(
        "hij,sjhe->sihe", score_gradient_part, key_row_block, preferred_element_type=jnp.float32
    )
    key_gradient_part = jnp.einsum(
        "hij,sihe->sjhe", score_gradient_part, query_row_block, preferred_element_type=jnp.float32
    )
    value_gradient_part = jnp.einsum(
        "hij,sihe->sjhe",
        attention_weight_rows,
        gradient_row_block,
        preferred_element_type=jnp.float32,
    )
    row_back = (
        lax.all_to_all(
            query_grad.astype(jnp.bfloat16).reshape(own_rows, cols, width),
            "col",
            split_axis=1,
            concat_axis=0,
            tiled=True,
        ),
        lax.all_to_all(
            key_gradient_part.astype(jnp.bfloat16).reshape(own_rows, cols, width),
            "col",
            split_axis=1,
            concat_axis=0,
            tiled=True,
        ),
        lax.all_to_all(
            value_gradient_part.astype(jnp.bfloat16).reshape(own_rows, cols, width),
            "col",
            split_axis=1,
            concat_axis=0,
            tiled=True,
        ),
    )
    flat_width = col_dev * width
    col_moved = (
        lax.all_to_all(
            col_query.reshape(seq_dev, flat_width), "seq", split_axis=1, concat_axis=0, tiled=True
        ),
        lax.all_to_all(
            col_key.reshape(seq_dev, flat_width), "seq", split_axis=1, concat_axis=0, tiled=True
        ),
        lax.all_to_all(
            col_value.reshape(seq_dev, flat_width), "seq", split_axis=1, concat_axis=0, tiled=True
        ),
        lax.all_to_all(
            col_grad.reshape(seq_dev, flat_width), "seq", split_axis=1, concat_axis=0, tiled=True
        ),
    )
    col_grads = column_core(
        split_heads(col_moved[0]),
        split_heads(col_moved[1]),
        split_heads(col_moved[2]),
        split_heads(col_moved[3]),
        col_scale,
    )
    share_width = col_moved[0].shape[1]
    col_back = (
        lax.all_to_all(
            col_grads[0].reshape(seqs, share_width), "seq", split_axis=0, concat_axis=1, tiled=True
        ),
        lax.all_to_all(
            col_grads[1].reshape(seqs, share_width), "seq", split_axis=0, concat_axis=1, tiled=True
        ),
        lax.all_to_all(
            col_grads[2].reshape(seqs, share_width), "seq", split_axis=0, concat_axis=1, tiled=True
        ),
    )
    return (
        row_back[0],
        row_back[1],
        row_back[2],
        col_back[0].reshape(seq_dev, col_dev, width),
        col_back[1].reshape(seq_dev, col_dev, width),
        col_back[2].reshape(seq_dev, col_dev, width),
    )


def solution(mesh):
    in_specs = (
        P(("grp", "seq"), "col", None),
        P(("grp", "seq"), "col", None),
        P(("grp", "seq"), "col", None),
        P(("grp", "seq"), "col", None),
        P(("grp", "seq"), "col", None),
        P(("grp", "seq"), "col", None),
        P(("grp", "seq"), "col", None),
        P(("grp", "seq"), "col", None),
    )
    out_specs = (
        P(("grp", "seq"), "col", None),
        P(("grp", "seq"), "col", None),
        P(("grp", "seq"), "col", None),
        P(("grp", "seq"), "col", None),
        P(("grp", "seq"), "col", None),
        P(("grp", "seq"), "col", None),
    )
    return jax.shard_map(local, mesh=mesh, in_specs=in_specs, out_specs=out_specs, check_vma=False)
```

profile of v0, /device:TPU:0, one launch (start us, length us, event | category | flops | bytes accessed | tf_op | source)
XLA Modules:
  0.0 195.9 jit_solution(17410516336404553708)
XLA Ops:
  0.6 1.6 copy.133
  2.3 4.3 %all-to-all-start.8 = ((bf16[32,4,768]{2,0,1:T(8,128)(2,1)}), bf16[32,4,768]{2,0,1:T(8,128)(2,1)S(1)}, u32[]{:S(2)}, u32[]{:S(2)}) async-start(bf16[32,4,768]{2,0,1:T(8,128)(2,1)} %copy.133), calls=%async_computation.8 | async-start | bytes 393216 | tf_op jit(solution)/shard_map/all_to_all | solution.py:123
  7.3 4.6 %all-to-all-done.8 = bf16[32,4,768]{2,0,1:T(8,128)(2,1)S(1)} async-done(((bf16[32,4,768]{2,0,1:T(8,128)(2,1)}), bf16[32,4,768]{2,0,1:T(8,128)(2,1)S(1)}, u32[]{:S(2)}, u32[]{:S(2)}) %all-to-all-start.8) | async-done | bytes 196640 | tf_op jit(solution)/shard_map/all_to_all | solution.py:123
  11.9 3.4 %all-to-all-start.9 = ((bf16[32,4,768]{2,0,1:T(8,128)(2,1)}), bf16[32,4,768]{2,0,1:T(8,128)(2,1)S(1)}, u32[]{:S(2)}, u32[]{:S(2)}) async-start(bf16[32,4,768]{2,0,1:T(8,128)(2,1)} %copy.136), calls=%async_computation.9 | async-start | bytes 393216 | tf_op jit(solution)/shard_map/all_to_all | solution.py:129
  16.0 4.6 %all-to-all-done.9 = bf16[32,4,768]{2,0,1:T(8,128)(2,1)S(1)} async-done(((bf16[32,4,768]{2,0,1:T(8,128)(2,1)}), bf16[32,4,768]{2,0,1:T(8,128)(2,1)S(1)}, u32[]{:S(2)}, u32[]{:S(2)}) %all-to-all-start.9) | async-done | bytes 196640 | tf_op jit(solution)/shard_map/all_to_all | solution.py:129
  20.6 3.4 %all-to-all-start.10 = ((bf16[32,4,768]{2,0,1:T(8,128)(2,1)}), bf16[32,4,768]{2,0,1:T(8,128)(2,1)S(1)}, u32[]{:S(2)}, u32[]{:S(2)}) async-start(bf16[32,4,768]{2,0,1:T(8,128)(2,1)} %copy.137), calls=%async_computation.10 | async-start | bytes 393216 | tf_op jit(solution)/shard_map/all_to_all | solution.py:126
  24.0 5.2 %all-to-all-done.10 = bf16[32,4,768]{2,0,1:T(8,128)(2,1)S(1)} async-done(((bf16[32,4,768]{2,0,1:T(8,128)(2,1)}), bf16[32,4,768]{2,0,1:T(8,128)(2,1)S(1)}, u32[]{:S(2)}, u32[]{:S(2)}) %all-to-all-start.10) | async-done | bytes 196640 | tf_op jit(solution)/shard_map/all_to_all | solution.py:126
  29.3 7.7 %all_to_all.214 = bf16[32,4,768]{2,0,1:T(8,128)(2,1)S(1)} all-to-all(bf16[32,4,768]{2,0,1:T(8,128)(2,1)S(1)} %copy.132), channel_id=1, replica_groups=mesh['grp'=2,'col'=4,'seq'=4] {'seq'}, dimensions={1} | all-to-all | bytes 393216 | tf_op jit(solution)/shard_map/all_to_all | solution.py:120
  37.0 12.7 %all_to_all.215 = bf16[32,4,768]{2,1,0:T(4,128)(2,1)S(1)} all-to-all(bf16[32,4,768]{2,1,0:T(4,128)(2,1)S(1)} %copy-done.3), channel_id=1, replica_groups=mesh['grp'=2,'col'=4,'seq'=4] {'col'}, dimensions={0} | all-to-all | bytes 393216 | tf_op jit(solution)/shard_map/all_to_all | solution.py:63
  49.7 3.4 %all-to-all-start.2 = ((bf16[32,4,768]{2,1,0:T(4,128)(2,1)}), bf16[32,4,768]{2,1,0:T(4,128)(2,1)S(1)}, u32[]{:S(2)}, u32[]{:S(2)}) async-start(bf16[32,4,768]{2,1,0:T(4,128)(2,1)} %param.11), calls=%async_computation.2 | async-start | bytes 393216 | tf_op jit(solution)/shard_map/all_to_all | solution.py:64
  55.8 3.5 %all-to-all-done.2 = bf16[32,4,768]{2,1,0:T(4,128)(2,1)S(1)} async-done(((bf16[32,4,768]{2,1,0:T(4,128)(2,1)}), bf16[32,4,768]{2,1,0:T(4,128)(2,1)S(1)}, u32[]{:S(2)}, u32[]{:S(2)}) %all-to-all-start.2) | async-done | bytes 196640 | tf_op jit(solution)/shard_map/all_to_all | solution.py:64
  59.4 3.4 %all-to-all-start.1 = ((bf16[32,4,768]{2,1,0:T(4,128)(2,1)}), bf16[32,4,768]{2,1,0:T(4,128)(2,1)S(1)}, u32[]{:S(2)}, u32[]{:S(2)}) async-start(bf16[32,4,768]{2,1,0:T(4,128)(2,1)} %param.9), calls=%async_computation.1 | async-start | bytes 393216 | tf_op jit(solution)/shard_map/all_to_all | solution.py:62
  63.5 5.4 %all-to-all-done.1 = bf16[32,4,768]{2,1,0:T(4,128)(2,1)S(1)} async-done(((bf16[32,4,768]{2,1,0:T(4,128)(2,1)}), bf16[32,4,768]{2,1,0:T(4,128)(2,1)S(1)}, u32[]{:S(2)}, u32[]{:S(2)}) %all-to-all-start.1) | async-done | bytes 196640 | tf_op jit(solution)/shard_map/all_to_all | solution.py:62
  68.9 3.4 %all-to-all-start = ((bf16[32,4,768]{2,1,0:T(4,128)(2,1)}), bf16[32,4,768]{2,1,0:T(4,128)(2,1)S(1)}, u32[]{:S(2)}, u32[]{:S(2)}) async-start(bf16[32,4,768]{2,1,0:T(4,128)(2,1)} %param.8), calls=%async_computation | async-start | bytes 393216 | tf_op jit(solution)/shard_map/all_to_all | solution.py:61
  73.1 1.0 all_to_all.191
  74.6 1.0 all_to_all.194
  76.6 1.0 all_to_all.197
  78.7 3.4 %all-to-all-start.11 = ((bf16[4,32,768]{2,1,0:T(8,128)(2,1)}), bf16[4,32,768]{2,1,0:T(8,128)(2,1)S(1)}, u32[]{:S(2)}, u32[]{:S(2)}) async-start(bf16[4,32,768]{2,1,0:T(8,128)(2,1)} %all_to_all.191), calls=%async_computation.11 | async-start | bytes 393216 | tf_op jit(solution)/shard_map/all_to_all | solution.py:142
  83.5 64.1 %all-reduce = (f32[12,16,16]{2,1,0:T(8,128)S(1)}, f32[12,16,16]{2,1,0:T(8,128)S(1)}) all-reduce(f32[12,16,16]{2,1,0:T(8,128)S(1)} %convolution_bitcast_fusion, f32[12,16,16]{2,1,0:T(8,128)S(1)} %fusion.21), channel_id=1, replica_groups=mesh['grp'=2,'col'=4,'seq'=4] {'col','seq'}, use_global_device_ids=true, to_apply=%region_3.0 | all-reduce | flops 6144 | bytes 49152 | tf_op jit(solution)/shard_map/psum | solution.py:81
  147.6 3.4 %all-to-all-start.12 = ((bf16[4,32,768]{2,1,0:T(8,128)(2,1)}), bf16[4,32,768]{2,1,0:T(8,128)(2,1)S(1)}, u32[]{:S(2)}, u32[]{:S(2)}) async-start(bf16[4,32,768]{2,1,0:T(8,128)(2,1)} %all_to_all.194), calls=%async_computation.12 | async-start | bytes 393216 | tf_op jit(solution)/shard_map/all_to_all | solution.py:145
  151.0 1.9 fusion.58
  152.9 3.4 %all-to-all-done.12 = bf16[4,32,768]{2,1,0:T(8,128)(2,1)S(1)} async-done(((bf16[4,32,768]{2,1,0:T(8,128)(2,1)}), bf16[4,32,768]{2,1,0:T(8,128)(2,1)S(1)}, u32[]{:S(2)}, u32[]{:S(2)}) %all-to-all-start.12) | async-done | bytes 196640 | tf_op jit(solution)/shard_map/all_to_all | solution.py:145
  156.3 3.4 %all-to-all-start.13 = ((bf16[4,32,768]{2,1,0:T(8,128)(2,1)}), bf16[4,32,768]{2,1,0:T(8,128)(2,1)S(1)}, u32[]{:S(2)}, u32[]{:S(2)}) async-start(bf16[4,32,768]{2,1,0:T(8,128)(2,1)} %all_to_all.197), calls=%async_computation.13 | async-start | bytes 393216 | tf_op jit(solution)/shard_map/all_to_all | solution.py:148
  160.7 1.0 reshape.116
  161.7 3.3 %all-to-all-done.13 = bf16[4,32,768]{2,1,0:T(8,128)(2,1)S(1)} async-done(((bf16[4,32,768]{2,1,0:T(8,128)(2,1)}), bf16[4,32,768]{2,1,0:T(8,128)(2,1)S(1)}, u32[]{:S(2)}, u32[]{:S(2)}) %all-to-all-start.13) | async-done | bytes 196640 | tf_op jit(solution)/shard_map/all_to_all | solution.py:148
  165.0 3.5 %all-to-all-start.4 = ((bf16[8,16,768]{2,0,1:T(8,128)(2,1)}), bf16[8,16,768]{2,0,1:T(8,128)(2,1)S(1)}, u32[]{:S(2)}, u32[]{:S(2)}) async-start(bf16[8,16,768]{2,0,1:T(8,128)(2,1)} %reshape.116), calls=%async_computation.4 | async-start | bytes 393216 | tf_op jit(solution)/shard_map/all_to_all | solution.py:96
  169.6 1.0 reshape.117
  170.6 5.3 %all-to-all-done.4 = bf16[8,16,768]{2,0,1:T(8,128)(2,1)S(1)} async-done(((bf16[8,16,768]{2,0,1:T(8,128)(2,1)}), bf16[8,16,768]{2,0,1:T(8,128)(2,1)S(1)}, u32[]{:S(2)}, u32[]{:S(2)}) %all-to-all-start.4) | async-done | bytes 196640 | tf_op jit(solution)/shard_map/all_to_all | solution.py:96
  175.9 3.4 %all-to-all-start.5 = ((bf16[8,16,768]{2,0,1:T(8,128)(2,1)}), bf16[8,16,768]{2,0,1:T(8,128)(2,1)S(1)}, u32[]{:S(2)}, u32[]{:S(2)}) async-start(bf16[8,16,768]{2,0,1:T(8,128)(2,1)} %reshape.117), calls=%async_computation.5 | async-start | bytes 393216 | tf_op jit(solution)/shard_map/all_to_all | solution.py:103
  181.3 4.2 %all-to-all-done.5 = bf16[8,16,768]{2,0,1:T(8,128)(2,1)S(1)} async-done(((bf16[8,16,768]{2,0,1:T(8,128)(2,1)}), bf16[8,16,768]{2,0,1:T(8,128)(2,1)S(1)}, u32[]{:S(2)}, u32[]{:S(2)}) %all-to-all-start.5) | async-done | bytes 196640 | tf_op jit(solution)/shard_map/all_to_all | solution.py:103
  185.5 3.4 %all-to-all-start.6 = ((bf16[8,16,768]{2,0,1:T(8,128)(2,1)}), bf16[8,16,768]{2,0,1:T(8,128)(2,1)S(1)}, u32[]{:S(2)}, u32[]{:S(2)}) async-start(bf16[8,16,768]{2,0,1:T(8,128)(2,1)} %reshape.118), calls=%async_computation.6 | async-start | bytes 393216 | tf_op jit(solution)/shard_map/all_to_all | solution.py:110
  193.1 2.0 %all-to-all-done.6 = bf16[8,16,768]{2,0,1:T(8,128)(2,1)S(1)} async-done(((bf16[8,16,768]{2,0,1:T(8,128)(2,1)}), bf16[8,16,768]{2,0,1:T(8,128)(2,1)S(1)}, u32[]{:S(2)}, u32[]{:S(2)}) %all-to-all-start.6) | async-done | bytes 196640 | tf_op jit(solution)/shard_map/all_to_all | solution.py:110
  (54 shorter events, 18.8 us)
Async XLA Ops:
  2.3 4.3 %copy-start = (bf16[32,4,768]{2,1,0:T(4,128)(2,1)S(1)}, bf16[32,4,768]{2,1,0:T(4,128)(2,1)}, u32[]{:S(2)}) copy-start(bf16[32,4,768]{2,1,0:T(4,128)(2,1)} %param.15) | copy-start | bytes 589828
  2.3 9.7 %all-to-all-start.8 = ((bf16[32,4,768]{2,0,1:T(8,128)(2,1)}), bf16[32,4,768]{2,0,1:T(8,128)(2,1)S(1)}, u32[]{:S(2)}, u32[]{:S(2)}) async-start(bf16[32,4,768]{2,0,1:T(8,128)(2,1)} %copy.133), calls=%async_computation.8 | async-start | bytes 393216 | tf_op jit(solution)/shard_map/all_to_all | solution.py:123
  7.3 8.0 %copy-start.1 = (bf16[32,4,768]{2,1,0:T(4,128)(2,1)S(1)}, bf16[32,4,768]{2,1,0:T(4,128)(2,1)}, u32[]{:S(2)}) copy-start(bf16[32,4,768]{2,1,0:T(4,128)(2,1)} %param.14) | copy-start | bytes 589828
  11.9 8.7 %all-to-all-start.9 = ((bf16[32,4,768]{2,0,1:T(8,128)(2,1)}), bf16[32,4,768]{2,0,1:T(8,128)(2,1)S(1)}, u32[]{:S(2)}, u32[]{:S(2)}) async-start(bf16[32,4,768]{2,0,1:T(8,128)(2,1)} %copy.136), calls=%async_computation.9 | async-start | bytes 393216 | tf_op jit(solution)/shard_map/all_to_all | solution.py:129
  16.0 8.0 %copy-start.2 = (bf16[32,4,768]{2,1,0:T(4,128)(2,1)S(1)}, bf16[32,4,768]{2,1,0:T(4,128)(2,1)}, u32[]{:S(2)}) copy-start(bf16[32,4,768]{2,1,0:T(4,128)(2,1)} %param.12) | copy-start | bytes 589828
  20.6 8.7 %all-to-all-start.10 = ((bf16[32,4,768]{2,0,1:T(8,128)(2,1)}), bf16[32,4,768]{2,0,1:T(8,128)(2,1)S(1)}, u32[]{:S(2)}, u32[]{:S(2)}) async-start(bf16[32,4,768]{2,0,1:T(8,128)(2,1)} %copy.137), calls=%async_computation.10 | async-start | bytes 393216 | tf_op jit(solution)/shard_map/all_to_all | solution.py:126
  24.0 13.0 %copy-start.3 = (bf16[32,4,768]{2,1,0:T(4,128)(2,1)S(1)}, bf16[32,4,768]{2,1,0:T(4,128)(2,1)}, u32[]{:S(2)}) copy-start(bf16[32,4,768]{2,1,0:T(4,128)(2,1)} %param.10) | copy-start | bytes 589828
  49.7 9.7 %all-to-all-start.2 = ((bf16[32,4,768]{2,1,0:T(4,128)(2,1)}), bf16[32,4,768]{2,1,0:T(4,128)(2,1)S(1)}, u32[]{:S(2)}, u32[]{:S(2)}) async-start(bf16[32,4,768]{2,1,0:T(4,128)(2,1)} %param.11), calls=%async_computation.2 | async-start | bytes 393216 | tf_op jit(solution)/shard_map/all_to_all | solution.py:64
  59.4 9.6 %all-to-all-start.1 = ((bf16[32,4,768]{2,1,0:T(4,128)(2,1)}), bf16[32,4,768]{2,1,0:T(4,128)(2,1)S(1)}, u32[]{:S(2)}, u32[]{:S(2)}) async-start(bf16[32,4,768]{2,1,0:T(4,128)(2,1)} %param.9), calls=%async_computation.1 | async-start | bytes 393216 | tf_op jit(solution)/shard_map/all_to_all | solution.py:62
  68.9 9.8 %all-to-all-start = ((bf16[32,4,768]{2,1,0:T(4,128)(2,1)}), bf16[32,4,768]{2,1,0:T(4,128)(2,1)S(1)}, u32[]{:S(2)}, u32[]{:S(2)}) async-start(bf16[32,4,768]{2,1,0:T(4,128)(2,1)} %param.8), calls=%async_computation | async-start | bytes 393216 | tf_op jit(solution)/shard_map/all_to_all | solution.py:61
  78.7 68.9 %all-to-all-start.11 = ((bf16[4,32,768]{2,1,0:T(8,128)(2,1)}), bf16[4,32,768]{2,1,0:T(8,128)(2,1)S(1)}, u32[]{:S(2)}, u32[]{:S(2)}) async-start(bf16[4,32,768]{2,1,0:T(8,128)(2,1)} %all_to_all.191), calls=%async_computation.11 | async-start | bytes 393216 | tf_op jit(solution)/shard_map/all_to_all | solution.py:142
  147.6 8.7 %all-to-all-start.12 = ((bf16[4,32,768]{2,1,0:T(8,128)(2,1)}), bf16[4,32,768]{2,1,0:T(8,128)(2,1)S(1)}, u32[]{:S(2)}, u32[]{:S(2)}) async-start(bf16[4,32,768]{2,1,0:T(8,128)(2,1)} %all_to_all.194), calls=%async_computation.12 | async-start | bytes 393216 | tf_op jit(solution)/shard_map/all_to_all | solution.py:145
  156.3 8.7 %all-to-all-start.13 = ((bf16[4,32,768]{2,1,0:T(8,128)(2,1)}), bf16[4,32,768]{2,1,0:T(8,128)(2,1)S(1)}, u32[]{:S(2)}, u32[]{:S(2)}) async-start(bf16[4,32,768]{2,1,0:T(8,128)(2,1)} %all_to_all.197), calls=%async_computation.13 | async-start | bytes 393216 | tf_op jit(solution)/shard_map/all_to_all | solution.py:148
  165.0 10.9 %all-to-all-start.4 = ((bf16[8,16,768]{2,0,1:T(8,128)(2,1)}), bf16[8,16,768]{2,0,1:T(8,128)(2,1)S(1)}, u32[]{:S(2)}, u32[]{:S(2)}) async-start(bf16[8,16,768]{2,0,1:T(8,128)(2,1)} %reshape.116), calls=%async_computation.4 | async-start | bytes 393216 | tf_op jit(solution)/shard_map/all_to_all | solution.py:96
  175.9 9.6 %all-to-all-start.5 = ((bf16[8,16,768]{2,0,1:T(8,128)(2,1)}), bf16[8,16,768]{2,0,1:T(8,128)(2,1)S(1)}, u32[]{:S(2)}, u32[]{:S(2)}) async-start(bf16[8,16,768]{2,0,1:T(8,128)(2,1)} %reshape.117), calls=%async_computation.5 | async-start | bytes 393216 | tf_op jit(solution)/shard_map/all_to_all | solution.py:103
  185.5 9.6 %all-to-all-start.6 = ((bf16[8,16,768]{2,0,1:T(8,128)(2,1)}), bf16[8,16,768]{2,0,1:T(8,128)(2,1)S(1)}, u32[]{:S(2)}, u32[]{:S(2)}) async-start(bf16[8,16,768]{2,0,1:T(8,128)(2,1)} %reshape.118), calls=%async_computation.6 | async-start | bytes 393216 | tf_op jit(solution)/shard_map/all_to_all | solution.py:110
where the time goes:
time: 197 us; the launch traced here: 196 us
  blocking collectives  84.5 us (43%)
  starting transfers between devices  41.6 us (21%)
  waiting for transfers between devices  41.6 us (21%)
  local copies, waits for them, and re-layouts  19.9 us (10%)
  matrix products  5.4 us (3%)
    psum x1, blocking collectives, local(): scores, prob_grad = lax.psum((score_part, prob_part), ('col', 'seq'))  64.1 us
    all_to_all x1, blocking collectives, local(): lax.all_to_all(row_value, 'col', split_axis=0, concat_axis=1, tiled=True)  12.7 us
    unnamed x18, local copies, waits for them, and re-layouts  8.05 us
    all_to_all x1, blocking collectives, local(): lax.all_to_all(col_query.reshape(seq_dev, flat_width), 'seq', split_axis=...  7.69 us
    all_to_all x1, waiting for transfers between devices, local(): lax.all_to_all(row_key, 'col', split_axis=0, concat_axis=1, tiled=True)  5.42 us
    all_to_all x1, waiting for transfers between devices, local(): lax.all_to_all(query_grad.astype(jnp.bfloat16).reshape(own_rows, cols, wi...  5.29 us
    all_to_all x1, waiting for transfers between devices, local(): lax.all_to_all(col_value.reshape(seq_dev, flat_width), 'seq', split_axis=...  5.25 us
    all_to_all x1, waiting for transfers between devices, local(): lax.all_to_all(col_key.reshape(seq_dev, flat_width), 'seq', split_axis=1,...  4.63 us
  transfers between devices with their start and end apart: 12, of which 10 were waited for; matrix products, arithmetic and copies ran while one was open for 11% of the time, Pallas kernels for 0%

commit v1 on v0

--- a/solution.py
+++ b/solution.py
@@ -5,6 +5,34 @@
 
 HEADS = 12
 HEAD = 64
+
+
+def proceed_cells(in_array, d_out, state):
+    a_next = in_array.shape
+    x_next = in_array.reshape(*a_next[:d_out], state, a_next[d_out] // state, *a_next[d_out + 1 :])
+    oldest = jnp.moveaxis(x_next, d_out, 0)
+    return oldest
+
+
+def supply_all_the_counts(inner_x, k_dim):
+    inner_x = jnp.moveaxis(inner_x, 0, k_dim)
+    row_out = inner_x.shape
+    state_now = inner_x.reshape(
+        *row_out[:k_dim], row_out[k_dim] * row_out[k_dim + 1], *row_out[k_dim + 2 :]
+    )
+    return state_now
+
+
+def point_the_sheets(local_array, device_axis, matrix, q_in):
+    extra, local_now = (lax.axis_size(device_axis), lax.axis_index(device_axis))
+    plain = proceed_cells(local_array, matrix, extra)
+    buffers = [plain[local_now]]
+    for u in tuple(range(1, extra)):
+        q_next = plain[local_now ^ u]
+        buffers.append(lax.ppermute(q_next, device_axis, [(it, it ^ u) for it in range(extra)]))
+    plain = jnp.stack(buffers, 0)[local_now ^ jnp.arange(extra)]
+    newest = supply_all_the_counts(plain, q_in)
+    return newest
 
 
 def tied_terms(scores, prob_grad, row_scale):
@@ -139,9 +167,7 @@
     )
     share_width = col_moved[0].shape[1]
     col_back = (
-        lax.all_to_all(
-            col_grads[0].reshape(seqs, share_width), "seq", split_axis=0, concat_axis=1, tiled=True
-        ),
+        point_the_sheets(col_grads[0].reshape(seqs, share_width), "seq", 0, 1),
         lax.all_to_all(
             col_grads[1].reshape(seqs, share_width), "seq", split_axis=0, concat_axis=1, tiled=True
         ),

time: 197 us -> 196 us (level)
  waiting for transfers between devices: 41.6 us -> 35.2 us
  matrix products: 5.4 us -> 9.11 us
  local copies, waits for them, and re-layouts: 19.9 us -> 21.9 us
    all_to_all x1 -> x0, starting transfers between devices: 3.38 us -> none  [local(): lax.all_to_all(col_grads[0].reshape(seqs, share_width), 'seq', split_axis...]
    all_to_all x1, waiting for transfers between devices: 3.37 us -> 0.01 us  [local(): lax.all_to_all(col_grads[1].reshape(seqs, share_width), 'seq', split_axis...]
    all_to_all x1, waiting for transfers between devices: 4.22 us -> 0.93 us  [local(): lax.all_to_all(key_gradient_part.astype(jnp.bfloat16).reshape(own_rows, c...]
    ppermute x0 -> x3, waiting for transfers between devices: none -> 2.7 us  [point_the_sheets(): lax.ppermute(q_next, device_axis, [(it, it ^ u) for it in range(extra)])]
    all_to_all x1, waiting for transfers between devices: 2.02 us -> 0.01 us  [local(): lax.all_to_all(value_gradient_part.astype(jnp.bfloat16).reshape(own_rows,...]
    unnamed x18 -> x36, local copies, waits for them, and re-layouts: 8.05 us -> 9.34 us
  transfers between devices with their start and end apart: 12 -> 14, of which waited for: 10 -> 10; matrix products, arithmetic and copies ran while one was open for 11% -> 14% of each run, Pallas kernels for 0% -> 0%
where the time goes in v1:
time: 196 us; the launch traced here: 195 us
  blocking collectives  84.6 us (43%)
  starting transfers between devices  40.8 us (21%)
  waiting for transfers between devices  35.2 us (18%)
  local copies, waits for them, and re-layouts  21.9 us (11%)
  matrix products  9.11 us (5%)
  other arithmetic  1.97 us (1%)
    psum x1, blocking collectives, local(): scores, prob_grad = lax.psum((score_part, prob_part), ('col', 'seq'))  64.2 us
    all_to_all x1, blocking collectives, local(): lax.all_to_all(row_value, 'col', split_axis=0, concat_axis=1, tiled=True)  12.7 us
    unnamed x36, local copies, waits for them, and re-layouts  9.34 us
    all_to_all x1, blocking collectives, local(): lax.all_to_all(col_query.reshape(seq_dev, flat_width), 'seq', split_axis=...  7.69 us
    all_to_all x1, waiting for transfers between devices, local(): lax.all_to_all(query_grad.astype(jnp.bfloat16).reshape(own_rows, cols, wi...  5.42 us
    all_to_all x1, waiting for transfers between devices, local(): lax.all_to_all(col_value.reshape(seq_dev, flat_width), 'seq', split_axis=...  5.25 us
    all_to_all x1, waiting for transfers between devices, local(): lax.all_to_all(row_grad, 'col', split_axis=0, concat_axis=1, tiled=True)  4.84 us
    all_to_all x1, waiting for transfers between devices, local(): lax.all_to_all(col_key.reshape(seq_dev, flat_width), 'seq', split_axis=1,...  4.63 us
  transfers between devices with their start and end apart: 14, of which 10 were waited for; matrix products, arithmetic and copies ran while one was open for 14% of the time, Pallas kernels for 0%

profile of v1, /device:TPU:0, one launch (start us, length us, event | category | flops | bytes accessed | tf_op | source)
XLA Modules:
  0.0 194.7 jit_solution(4754480474658435658)
XLA Ops:
  0.6 1.6 copy.132
  2.3 4.3 %all-to-all-start.8 = ((bf16[32,4,768]{2,0,1:T(8,128)(2,1)}), bf16[32,4,768]{2,0,1:T(8,128)(2,1)S(1)}, u32[]{:S(2)}, u32[]{:S(2)}) async-start(bf16[32,4,768]{2,0,1:T(8,128)(2,1)} %copy.132), calls=%async_computation.8 | async-start | bytes 393216 | tf_op jit(solution)/shard_map/all_to_all | solution.py:151
  7.3 4.6 %all-to-all-done.8 = bf16[32,4,768]{2,0,1:T(8,128)(2,1)S(1)} async-done(((bf16[32,4,768]{2,0,1:T(8,128)(2,1)}), bf16[32,4,768]{2,0,1:T(8,128)(2,1)S(1)}, u32[]{:S(2)}, u32[]{:S(2)}) %all-to-all-start.8) | async-done | bytes 196640 | tf_op jit(solution)/shard_map/all_to_all | solution.py:151
  11.9 3.4 %all-to-all-start.9 = ((bf16[32,4,768]{2,0,1:T(8,128)(2,1)}), bf16[32,4,768]{2,0,1:T(8,128)(2,1)S(1)}, u32[]{:S(2)}, u32[]{:S(2)}) async-start(bf16[32,4,768]{2,0,1:T(8,128)(2,1)} %copy.135), calls=%async_computation.9 | async-start | bytes 393216 | tf_op jit(solution)/shard_map/all_to_all | solution.py:157
  16.0 4.6 %all-to-all-done.9 = bf16[32,4,768]{2,0,1:T(8,128)(2,1)S(1)} async-done(((bf16[32,4,768]{2,0,1:T(8,128)(2,1)}), bf16[32,4,768]{2,0,1:T(8,128)(2,1)S(1)}, u32[]{:S(2)}, u32[]{:S(2)}) %all-to-all-start.9) | async-done | bytes 196640 | tf_op jit(solution)/shard_map/all_to_all | solution.py:157
  20.6 3.4 %all-to-all-start.10 = ((bf16[32,4,768]{2,0,1:T(8,128)(2,1)}), bf16[32,4,768]{2,0,1:T(8,128)(2,1)S(1)}, u32[]{:S(2)}, u32[]{:S(2)}) async-start(bf16[32,4,768]{2,0,1:T(8,128)(2,1)} %copy.136), calls=%async_computation.10 | async-start | bytes 393216 | tf_op jit(solution)/shard_map/all_to_all | solution.py:154
  24.0 5.2 %all-to-all-done.10 = bf16[32,4,768]{2,0,1:T(8,128)(2,1)S(1)} async-done(((bf16[32,4,768]{2,0,1:T(8,128)(2,1)}), bf16[32,4,768]{2,0,1:T(8,128)(2,1)S(1)}, u32[]{:S(2)}, u32[]{:S(2)}) %all-to-all-start.10) | async-done | bytes 196640 | tf_op jit(solution)/shard_map/all_to_all | solution.py:154
  29.3 7.7 %all_to_all.198 = bf16[32,4,768]{2,0,1:T(8,128)(2,1)S(1)} all-to-all(bf16[32,4,768]{2,0,1:T(8,128)(2,1)S(1)} %copy.131), channel_id=1, replica_groups=mesh['grp'=2,'col'=4,'seq'=4] {'seq'}, dimensions={1} | all-to-all | bytes 393216 | tf_op jit(solution)/shard_map/all_to_all | solution.py:148
  37.0 12.7 %all_to_all.199 = bf16[32,4,768]{2,1,0:T(4,128)(2,1)S(1)} all-to-all(bf16[32,4,768]{2,1,0:T(4,128)(2,1)S(1)} %copy-done.8), channel_id=1, replica_groups=mesh['grp'=2,'col'=4,'seq'=4] {'col'}, dimensions={0} | all-to-all | bytes 393216 | tf_op jit(solution)/shard_map/all_to_all | solution.py:91
  49.7 3.4 %all-to-all-start.2 = ((bf16[32,4,768]{2,1,0:T(4,128)(2,1)}), bf16[32,4,768]{2,1,0:T(4,128)(2,1)S(1)}, u32[]{:S(2)}, u32[]{:S(2)}) async-start(bf16[32,4,768]{2,1,0:T(4,128)(2,1)} %param.11), calls=%async_computation.2 | async-start | bytes 393216 | tf_op jit(solution)/shard_map/all_to_all | solution.py:92
  54.5 4.8 %all-to-all-done.2 = bf16[32,4,768]{2,1,0:T(4,128)(2,1)S(1)} async-done(((bf16[32,4,768]{2,1,0:T(4,128)(2,1)}), bf16[32,4,768]{2,1,0:T(4,128)(2,1)S(1)}, u32[]{:S(2)}, u32[]{:S(2)}) %all-to-all-start.2) | async-done | bytes 196640 | tf_op jit(solution)/shard_map/all_to_all | solution.py:92
  59.4 3.4 %all-to-all-start.1 = ((bf16[32,4,768]{2,1,0:T(4,128)(2,1)}), bf16[32,4,768]{2,1,0:T(4,128)(2,1)S(1)}, u32[]{:S(2)}, u32[]{:S(2)}) async-start(bf16[32,4,768]{2,1,0:T(4,128)(2,1)} %param.9), calls=%async_computation.1 | async-start | bytes 393216 | tf_op jit(solution)/shard_map/all_to_all | solution.py:90
  62.7 1.3 fusion.60
  65.4 3.6 %all-to-all-done.1 = bf16[32,4,768]{2,1,0:T(4,128)(2,1)S(1)} async-done(((bf16[32,4,768]{2,1,0:T(4,128)(2,1)}), bf16[32,4,768]{2,1,0:T(4,128)(2,1)S(1)}, u32[]{:S(2)}, u32[]{:S(2)}) %all-to-all-start.1) | async-done | bytes 196640 | tf_op jit(solution)/shard_map/all_to_all | solution.py:90
  68.9 3.4 %all-to-all-start = ((bf16[32,4,768]{2,1,0:T(4,128)(2,1)}), bf16[32,4,768]{2,1,0:T(4,128)(2,1)S(1)}, u32[]{:S(2)}, u32[]{:S(2)}) async-start(bf16[32,4,768]{2,1,0:T(4,128)(2,1)} %param.8), calls=%async_computation | async-start | bytes 393216 | tf_op jit(solution)/shard_map/all_to_all | solution.py:89
  72.3 1.8 fusion.13
  77.6 1.1 reshape.112
  79.5 3.4 %all-to-all-start.11 = ((bf16[4,32,768]{2,1,0:T(8,128)(2,1)}), bf16[4,32,768]{2,1,0:T(8,128)(2,1)S(1)}, u32[]{:S(2)}, u32[]{:S(2)}) async-start(bf16[4,32,768]{2,1,0:T(8,128)(2,1)} %all_to_all.179), calls=%async_computation.11 | async-start | bytes 393216 | tf_op jit(solution)/shard_map/all_to_all | solution.py:171
  85.0 64.2 %all-reduce = (f32[12,16,16]{2,1,0:T(8,128)S(1)}, f32[12,16,16]{2,1,0:T(8,128)S(1)}) all-reduce(f32[12,16,16]{2,1,0:T(8,128)S(1)} %convolution_bitcast_fusion, f32[12,16,16]{2,1,0:T(8,128)S(1)} %fusion.21), channel_id=1, replica_groups=mesh['grp'=2,'col'=4,'seq'=4] {'col','seq'}, use_global_device_ids=true, to_apply=%region_3.0 | all-reduce | flops 6144 | bytes 49152 | tf_op jit(solution)/shard_map/psum | solution.py:109
  149.3 1.9 fusion.59
  151.2 3.4 %all-to-all-start.12 = ((bf16[4,32,768]{2,1,0:T(8,128)(2,1)}), bf16[4,32,768]{2,1,0:T(8,128)(2,1)S(1)}, u32[]{:S(2)}, u32[]{:S(2)}) async-start(bf16[4,32,768]{2,1,0:T(8,128)(2,1)} %all_to_all.182), calls=%async_computation.12 | async-start | bytes 393216 | tf_op jit(solution)/shard_map/all_to_all | solution.py:174
  155.7 1.0 reshape.133
  156.7 3.3 %all-to-all-done.12 = bf16[4,32,768]{2,1,0:T(8,128)(2,1)S(1)} async-done(((bf16[4,32,768]{2,1,0:T(8,128)(2,1)}), bf16[4,32,768]{2,1,0:T(8,128)(2,1)S(1)}, u32[]{:S(2)}, u32[]{:S(2)}) %all-to-all-start.12) | async-done | bytes 196640 | tf_op jit(solution)/shard_map/all_to_all | solution.py:174
  159.9 3.4 %all-to-all-start.4 = ((bf16[8,16,768]{2,0,1:T(8,128)(2,1)}), bf16[8,16,768]{2,0,1:T(8,128)(2,1)S(1)}, u32[]{:S(2)}, u32[]{:S(2)}) async-start(bf16[8,16,768]{2,0,1:T(8,128)(2,1)} %reshape.133), calls=%async_computation.4 | async-start | bytes 393216 | tf_op jit(solution)/shard_map/all_to_all | solution.py:124
  164.5 1.0 reshape.134
  165.5 5.4 %all-to-all-done.4 = bf16[8,16,768]{2,0,1:T(8,128)(2,1)S(1)} async-done(((bf16[8,16,768]{2,0,1:T(8,128)(2,1)}), bf16[8,16,768]{2,0,1:T(8,128)(2,1)S(1)}, u32[]{:S(2)}, u32[]{:S(2)}) %all-to-all-start.4) | async-done | bytes 196640 | tf_op jit(solution)/shard_map/all_to_all | solution.py:124
  170.9 3.5 %all-to-all-start.5 = ((bf16[8,16,768]{2,0,1:T(8,128)(2,1)}), bf16[8,16,768]{2,0,1:T(8,128)(2,1)S(1)}, u32[]{:S(2)}, u32[]{:S(2)}) async-start(bf16[8,16,768]{2,0,1:T(8,128)(2,1)} %reshape.134), calls=%async_computation.5 | async-start | bytes 393216 | tf_op jit(solution)/shard_map/all_to_all | solution.py:131
  174.5 1.7 fusion.15
  180.5 3.9 %all-to-all-start.6 = ((bf16[8,16,768]{2,0,1:T(8,128)(2,1)}), bf16[8,16,768]{2,0,1:T(8,128)(2,1)S(1)}, u32[]{:S(2)}, u32[]{:S(2)}) async-start(bf16[8,16,768]{2,0,1:T(8,128)(2,1)} %reshape.135), calls=%async_computation.6 | async-start | bytes 393216 | tf_op jit(solution)/shard_map/all_to_all | solution.py:138
  185.2 1.2 collective-permute-start
  186.4 1.6 collective-permute-done.2
  188.0 1.1 collective-permute-done.1
  (81 shorter events, 23.2 us)
Async XLA Ops:
  2.3 4.3 %copy-start.5 = (bf16[32,4,768]{2,1,0:T(4,128)(2,1)S(1)}, bf16[32,4,768]{2,1,0:T(4,128)(2,1)}, u32[]{:S(2)}) copy-start(bf16[32,4,768]{2,1,0:T(4,128)(2,1)} %param.15) | copy-start | bytes 589828
  2.3 9.7 %all-to-all-start.8 = ((bf16[32,4,768]{2,0,1:T(8,128)(2,1)}), bf16[32,4,768]{2,0,1:T(8,128)(2,1)S(1)}, u32[]{:S(2)}, u32[]{:S(2)}) async-start(bf16[32,4,768]{2,0,1:T(8,128)(2,1)} %copy.132), calls=%async_computation.8 | async-start | bytes 393216 | tf_op jit(solution)/shard_map/all_to_all | solution.py:151
  7.3 8.0 %copy-start.6 = (bf16[32,4,768]{2,1,0:T(4,128)(2,1)S(1)}, bf16[32,4,768]{2,1,0:T(4,128)(2,1)}, u32[]{:S(2)}) copy-start(bf16[32,4,768]{2,1,0:T(4,128)(2,1)} %param.14) | copy-start | bytes 589828
  11.9 8.7 %all-to-all-start.9 = ((bf16[32,4,768]{2,0,1:T(8,128)(2,1)}), bf16[32,4,768]{2,0,1:T(8,128)(2,1)S(1)}, u32[]{:S(2)}, u32[]{:S(2)}) async-start(bf16[32,4,768]{2,0,1:T(8,128)(2,1)} %copy.135), calls=%async_computation.9 | async-start | bytes 393216 | tf_op jit(solution)/shard_map/all_to_all | solution.py:157
  16.0 8.0 %copy-start.7 = (bf16[32,4,768]{2,1,0:T(4,128)(2,1)S(1)}, bf16[32,4,768]{2,1,0:T(4,128)(2,1)}, u32[]{:S(2)}) copy-start(bf16[32,4,768]{2,1,0:T(4,128)(2,1)} %param.12) | copy-start | bytes 589828
  20.6 8.7 %all-to-all-start.10 = ((bf16[32,4,768]{2,0,1:T(8,128)(2,1)}), bf16[32,4,768]{2,0,1:T(8,128)(2,1)S(1)}, u32[]{:S(2)}, u32[]{:S(2)}) async-start(bf16[32,4,768]{2,0,1:T(8,128)(2,1)} %copy.136), calls=%async_computation.10 | async-start | bytes 393216 | tf_op jit(solution)/shard_map/all_to_all | solution.py:154
  24.0 13.0 %copy-start.8 = (bf16[32,4,768]{2,1,0:T(4,128)(2,1)S(1)}, bf16[32,4,768]{2,1,0:T(4,128)(2,1)}, u32[]{:S(2)}) copy-start(bf16[32,4,768]{2,1,0:T(4,128)(2,1)} %param.10) | copy-start | bytes 589828
  49.7 9.7 %all-to-all-start.2 = ((bf16[32,4,768]{2,1,0:T(4,128)(2,1)}), bf16[32,4,768]{2,1,0:T(4,128)(2,1)S(1)}, u32[]{:S(2)}, u32[]{:S(2)}) async-start(bf16[32,4,768]{2,1,0:T(4,128)(2,1)} %param.11), calls=%async_computation.2 | async-start | bytes 393216 | tf_op jit(solution)/shard_map/all_to_all | solution.py:92
  53.8 21.7 %copy-start.9 = (bf16[128,12,64]{0,2,1:T(8,128)(2,1)}, bf16[128,12,64]{0,2,1:T(8,128)(2,1)S(1)}, u32[]{:S(2)}) copy-start(bf16[128,12,64]{0,2,1:T(8,128)(2,1)S(1)} %copy.134) | copy-start | bytes 589828
  59.4 9.6 %all-to-all-start.1 = ((bf16[32,4,768]{2,1,0:T(4,128)(2,1)}), bf16[32,4,768]{2,1,0:T(4,128)(2,1)S(1)}, u32[]{:S(2)}, u32[]{:S(2)}) async-start(bf16[32,4,768]{2,1,0:T(4,128)(2,1)} %param.9), calls=%async_computation.1 | async-start | bytes 393216 | tf_op jit(solution)/shard_map/all_to_all | solution.py:90
  64.0 11.5 %copy-start.11 = (f32[12,128]{1,0:T(8,128)}, f32[12,128]{1,0:T(8,128)S(1)}, u32[]{:S(2)}) copy-start(f32[12,128]{1,0:T(8,128)S(1)} %get-tuple-element.32) | copy-start | bytes 18436
  68.9 10.5 %all-to-all-start = ((bf16[32,4,768]{2,1,0:T(4,128)(2,1)}), bf16[32,4,768]{2,1,0:T(4,128)(2,1)S(1)}, u32[]{:S(2)}, u32[]{:S(2)}) async-start(bf16[32,4,768]{2,1,0:T(4,128)(2,1)} %param.8), calls=%async_computation | async-start | bytes 393216 | tf_op jit(solution)/shard_map/all_to_all | solution.py:89
  79.5 5.0 %copy-start = (bf16[8,16,12,64]{3,2,0,1:T(8,128)(2,1)}, bf16[8,16,12,64]{3,2,0,1:T(8,128)(2,1)S(1)}, u32[]{:S(2)}) copy-start(bf16[8,16,12,64]{3,2,0,1:T(8,128)(2,1)S(1)} %reshape.110) | copy-start | bytes 589828
  79.5 71.7 %all-to-all-start.11 = ((bf16[4,32,768]{2,1,0:T(8,128)(2,1)}), bf16[4,32,768]{2,1,0:T(8,128)(2,1)S(1)}, u32[]{:S(2)}, u32[]{:S(2)}) async-start(bf16[4,32,768]{2,1,0:T(8,128)(2,1)} %all_to_all.179), calls=%async_computation.11 | async-start | bytes 393216 | tf_op jit(solution)/shard_map/all_to_all | solution.py:171
  82.9 1.0 copy-start.2
  85.0 69.6 %copy-start.1 = (bf16[8,16,12,64]{3,2,0,1:T(8,128)(2,1)S(1)}, bf16[8,16,12,64]{3,2,0,1:T(8,128)(2,1)}, u32[]{:S(2)}) copy-start(bf16[8,16,12,64]{3,2,0,1:T(8,128)(2,1)} %copy-done) | copy-start | bytes 589828
  149.2 1.9 copy-start.3
  151.2 8.7 %all-to-all-start.12 = ((bf16[4,32,768]{2,1,0:T(8,128)(2,1)}), bf16[4,32,768]{2,1,0:T(8,128)(2,1)S(1)}, u32[]{:S(2)}, u32[]{:S(2)}) async-start(bf16[4,32,768]{2,1,0:T(8,128)(2,1)} %all_to_all.182), calls=%async_computation.12 | async-start | bytes 393216 | tf_op jit(solution)/shard_map/all_to_all | solution.py:174
  159.9 10.9 %all-to-all-start.4 = ((bf16[8,16,768]{2,0,1:T(8,128)(2,1)}), bf16[8,16,768]{2,0,1:T(8,128)(2,1)S(1)}, u32[]{:S(2)}, u32[]{:S(2)}) async-start(bf16[8,16,768]{2,0,1:T(8,128)(2,1)} %reshape.133), calls=%async_computation.4 | async-start | bytes 393216 | tf_op jit(solution)/shard_map/all_to_all | solution.py:124
  165.5 9.0 %copy-start.10 = (bf16[128,12,64]{0,2,1:T(8,128)(2,1)S(1)}, bf16[128,12,64]{0,2,1:T(8,128)(2,1)}, u32[]{:S(2)}) copy-start(bf16[128,12,64]{0,2,1:T(8,128)(2,1)} %copy-done.9) | copy-start | bytes 589828
  165.5 9.0 %copy-start.12 = (f32[12,128]{1,0:T(8,128)S(1)}, f32[12,128]{1,0:T(8,128)}, u32[]{:S(2)}) copy-start(f32[12,128]{1,0:T(8,128)} %copy-done.11) | copy-start | bytes 18436
  170.9 9.6 %all-to-all-start.5 = ((bf16[8,16,768]{2,0,1:T(8,128)(2,1)}), bf16[8,16,768]{2,0,1:T(8,128)(2,1)S(1)}, u32[]{:S(2)}, u32[]{:S(2)}) async-start(bf16[8,16,768]{2,0,1:T(8,128)(2,1)} %reshape.134), calls=%async_computation.5 | async-start | bytes 393216 | tf_op jit(solution)/shard_map/all_to_all | solution.py:131
  176.7 0.9 copy-start.4
  180.5 13.4 %all-to-all-start.6 = ((bf16[8,16,768]{2,0,1:T(8,128)(2,1)}), bf16[8,16,768]{2,0,1:T(8,128)(2,1)S(1)}, u32[]{:S(2)}, u32[]{:S(2)}) async-start(bf16[8,16,768]{2,0,1:T(8,128)(2,1)} %reshape.135), calls=%async_computation.6 | async-start | bytes 393216 | tf_op jit(solution)/shard_map/all_to_all | solution.py:138
  184.4 3.6 %collective-permute-start.2 = (bf16[32,768]{1,0:T(8,128)(2,1)S(1)}, bf16[32,768]{1,0:T(8,128)(2,1)S(1)}, u32[]{:S(2)}, u32[]{:S(2)}) collective-permute-start(bf16[32,768]{1,0:T(8,128)(2,1)S(1)} %get-tuple-element.27), channel_id=1, source_target_pairs={{0,3},{1,2},{2,1},{3,0},{4,7},{5,6},{6,5},{7,4},{8,11},{9,10},{10,... | collective-permute-start | bytes 147464 | tf_op jit(solution)/shard_map/ppermute | solution.py:32
  184.5 4.6 %collective-permute-start.1 = (bf16[32,768]{1,0:T(8,128)(2,1)S(1)}, bf16[32,768]{1,0:T(8,128)(2,1)S(1)}, u32[]{:S(2)}, u32[]{:S(2)}) collective-permute-start(bf16[32,768]{1,0:T(8,128)(2,1)S(1)} %get-tuple-element.28), channel_id=1, source_target_pairs={{0,2},{1,3},{2,0},{3,1},{4,6},{5,7},{6,4},{7,5},{8,10},{9,11},{10,... | collective-permute-start | bytes 147464 | tf_op jit(solution)/shard_map/ppermute | solution.py:32
  185.2 3.9 %collective-permute-start = (bf16[32,768]{1,0:T(8,128)(2,1)S(1)}, bf16[32,768]{1,0:T(8,128)(2,1)S(1)}, u32[]{:S(2)}, u32[]{:S(2)}) collective-permute-start(bf16[32,768]{1,0:T(8,128)(2,1)S(1)} %get-tuple-element.29), channel_id=1, source_target_pairs={{0,1},{1,0},{2,3},{3,2},{4,5},{5,4},{6,7},{7,6},{8,9},{9,8},{10,11... | collective-permute-start | bytes 147464 | tf_op jit(solution)/shard_map/ppermute | solution.py:32
